TPU v7x, 32 devices: a whole 2x2x4 slice. The times are simulated.
32 devices in a mesh: node: 8 (over z, x), feat: 4 (over y, core).
Axes of the slice: x: 2, y: 2, z: 4, core: 2. Of those that a mesh axis runs over, the one named last changes fastest.
Arguments:
- features: bfloat16 [256, 4096], P('feat', 'node'), may hold values from -6 to 6
- tile_values: bfloat16 [256, 128, 128], P('node'), may hold values from -0.1875 to 0.1875
- tile_rows: int32 [64, 4], P('node'), may hold values from 0 to 3
- tile_cols: int32 [64, 4], P('node'), may hold values from 0 to 3
- tile_counts: int32 [64], P('node'), may hold values from 0 to 4, as said below
- weight: bfloat16 [256, 256], replicated, may hold values from -0.375 to 0.375
- cotangent: bfloat16 [256, 4096], P(None, ('node', 'feat')), may hold values from -6 to 6
Outputs:
- activated: bfloat16 [256, 4096], P(None, ('node', 'feat'))
- grad_weight: float32 [256, 256], replicated
- grad_features: float32 [256, 4096], P('feat', 'node')
Inputs may be any that keep to these rules, and one draw needn't show every extreme that they name: `tile_counts`: slots at or past a pair's count are ignored; some pair has all 4 slots live, and the live slots of one receiving node index vary strongly between indices.
All inputs are finite; a program needn't handle non-finite values.
Results may differ from a plain program's by a relative error of at most 0.012.
Values may be sent and summed in bfloat16 or wider, within the bound.
No kernel may reach another device: no remote copies, remote signals or barrier semaphores. Data moves between devices by JAX's collectives and lax.ppermute only.
A program may use at most 64 MiB of HBM per device.

v0:
```python
import jax
import jax.numpy as jnp
from jax import lax
from jax.sharding import PartitionSpec as P


def passed_along(x, axis, by):
    count = lax.axis_size(axis)
    return lax.ppermute(x, axis, [(i, (i + by) % count) for i in range(count)])


def select_pair(tile_values, tile_rows, tile_cols, tile_counts, source):
    slots = tile_rows.shape[1]
    values = lax.dynamic_slice_in_dim(tile_values, source * slots, slots, 0)
    row_ids = lax.dynamic_index_in_dim(tile_rows, source, 0, keepdims=False)
    col_ids = lax.dynamic_index_in_dim(tile_cols, source, 0, keepdims=False)
    number = lax.dynamic_index_in_dim(tile_counts, source, 0, keepdims=False)
    live = (jnp.arange(slots) < number).astype(jnp.float32)
    return (values, row_ids, col_ids, live)


def add_forward(totals, piece, parts, keep):
    values, row_ids, col_ids, live = parts
    blocks_in = piece.reshape(piece.shape[0], -1, values.shape[1])
    block_count = blocks_in.shape[1]
    pick = jax.nn.one_hot(col_ids, block_count, dtype=jnp.bfloat16)
    chosen = jnp.einsum("frm,sr->fsm", blocks_in, pick, preferred_element_type=jnp.float32).astype(
        jnp.bfloat16
    )
    product = jnp.einsum("fsm,sjm->fsj", chosen, values, preferred_element_type=jnp.float32)
    place = jax.nn.one_hot(row_ids, block_count, dtype=jnp.float32) * (live * keep)[:, None]
    return totals + jnp.einsum("fsj,sr->frj", product, place)


def add_backward(totals, grad_blocks, parts, keep):
    values, row_ids, col_ids, live = parts
    block_count = grad_blocks.shape[1]
    pick = jax.nn.one_hot(row_ids, block_count, dtype=jnp.bfloat16)
    chosen = jnp.einsum(
        "frj,sr->fsj", grad_blocks, pick, preferred_element_type=jnp.float32
    ).astype(jnp.bfloat16)
    product = jnp.einsum("fsj,sjm->fsm", chosen, values, preferred_element_type=jnp.float32)
    place = jax.nn.one_hot(col_ids, block_count, dtype=jnp.float32) * (live * keep)[:, None]
    return totals + jnp.einsum("fsm,sc->fcm", product, place)


def per_device(features, tile_values, tile_rows, tile_cols, tile_counts, weight, cotangent):
    node_count = lax.axis_size("node")
    own_index = lax.axis_index("node")
    slice_width = features.shape[0]
    local_nodes = features.shape[1]
    tile_side = tile_values.shape[1]
    block_count = local_nodes // tile_side

    def pair_of(source):
        return select_pair(tile_values, tile_rows, tile_cols, tile_counts, source)

    totals = jnp.zeros((slice_width, block_count, tile_side), jnp.float32)
    totals = add_forward(totals, features, pair_of(own_index), 1.0)

    def ahead_step(step, carry):
        running, moving = carry
        moving = passed_along(moving, "node", 1)
        source = (own_index - step) % node_count
        return (add_forward(running, moving, pair_of(source), 1.0), moving)

    totals, _ = lax.fori_loop(1, node_count, ahead_step, (totals, features))
    aggregated = totals.reshape(slice_width, local_nodes).astype(jnp.bfloat16)
    full_rows = lax.all_to_all(aggregated, "feat", split_axis=1, concat_axis=0, tiled=True)
    pre = jnp.dot(weight.T, full_rows, preferred_element_type=jnp.float32)
    activated = jax.nn.silu(pre).astype(jnp.bfloat16)
    sigma = jax.nn.sigmoid(pre)
    dpre = (cotangent.astype(jnp.float32) * sigma * (1.0 + pre * (1.0 - sigma))).astype(
        jnp.bfloat16
    )
    weight_part = lax.dot_general(
        full_rows, dpre, (((1,), (1,)), ((), ())), preferred_element_type=jnp.float32
    )
    grad_weight = lax.psum(weight_part, ("node", "feat"))
    dagg = jnp.dot(weight, dpre, preferred_element_type=jnp.float32).astype(jnp.bfloat16)
    grad_slices = lax.all_to_all(dagg, "feat", split_axis=0, concat_axis=1, tiled=True)
    grad_blocks = grad_slices.reshape(slice_width, block_count, tile_side)
    zeros = jnp.zeros((slice_width, block_count, tile_side), jnp.float32)
    start = add_backward(zeros, grad_blocks, pair_of((own_index - 1) % node_count), 1.0)

    def carry_step(step, running):
        running = passed_along(running, "node", 1)
        owner = (own_index - step - 1) % node_count
        return add_backward(running, grad_blocks, pair_of(owner), 1.0)

    gradient = lax.fori_loop(1, node_count, carry_step, start)
    return (activated, grad_weight, gradient.reshape(slice_width, local_nodes))


def solution(mesh):
    placed = (
        P("feat", "node"),
        P("node", None, None),
        P("node", None),
        P("node", None),
        P("node"),
        P(),
        P(None, ("node", "feat")),
    )
    return jax.shard_map(
        per_device,
        mesh=mesh,
        in_specs=placed,
        out_specs=(P(None, ("node", "feat")), P(), P("feat", "node")),
        check_vma=False,
    )
```

profile of v0, /device:TPU:0, one launch (start us, length us, event | category | flops | bytes accessed | tf_op | source)
XLA Modules:
  0.0 227.0 jit_solution(9543807741233657913)
XLA Ops:
  11.7 1.1 fusion.47
  12.9 62.7 %while.32 = (s32[]{:T(128)}, f32[64,4,128]{2,1,0:T(4,128)S(1)}, bf16[64,512]{1,0:T(8,128)(2,1)S(1)}, s32[]{:T(128)}, s32[8,4]{1,0:T(8,128)S(1)}, /*index=5*/s32[...) while((s32[]{:T(128)}, f32[64,4,128]{2,1,0:T(4,128)S(1)}, ...), condition=%wide.region_1.2_spmd, body=%wide.region_0.1_spmd.sunk | while | flops 8945741 | bytes 1245694 | solution.py:67
  12.9 3.0 %collective-permute-start = (bf16[64,512]{1,0:T(8,128)(2,1)S(1)}, bf16[64,512]{1,0:T(8,128)(2,1)S(1)}, u32[]{:S(2)}, u32[]{:S(2)}) collective-permute-start(bf16[64,512]{1,0:T(8,128)(2,1)S(1)} %get-tuple-element.610), channel_id=1, source_target_pairs={{0,4},{4,8},{8,12},{12,16},{16,20},{20,24},{24,28},{28,0},{1,5},{5... | collective-permute-start | bytes 196616 | tf_op jit(solution)/shard_map/while/body/eval_jaxpr/ppermute | solution.py:9
  17.2 4.0 %collective-permute-done = bf16[64,512]{1,0:T(8,128)(2,1)S(1)} collective-permute-done((bf16[64,512]{1,0:T(8,128)(2,1)S(1)}, bf16[64,512]{1,0:T(8,128)(2,1)S(1)}, u32[]{:S(2)}, u32[]{:S(2)}) %collective-permute-start) | collective-permute-done | bytes 65568 | tf_op jit(solution)/shard_map/while/body/eval_jaxpr/ppermute | solution.py:9
  21.5 1.1 fusion.115
  24.3 5.7 %collective-permute-done = bf16[64,512]{1,0:T(8,128)(2,1)S(1)} collective-permute-done((bf16[64,512]{1,0:T(8,128)(2,1)S(1)}, bf16[64,512]{1,0:T(8,128)(2,1)S(1)}, u32[]{:S(2)}, u32[]{:S(2)}) %collective-permute-start) | collective-permute-done | bytes 65568 | tf_op jit(solution)/shard_map/while/body/eval_jaxpr/ppermute | solution.py:9
  30.3 1.1 fusion.115
  33.1 5.7 %collective-permute-done = bf16[64,512]{1,0:T(8,128)(2,1)S(1)} collective-permute-done((bf16[64,512]{1,0:T(8,128)(2,1)S(1)}, bf16[64,512]{1,0:T(8,128)(2,1)S(1)}, u32[]{:S(2)}, u32[]{:S(2)}) %collective-permute-start) | collective-permute-done | bytes 65568 | tf_op jit(solution)/shard_map/while/body/eval_jaxpr/ppermute | solution.py:9
  39.0 1.1 fusion.115
  41.9 5.7 %collective-permute-done = bf16[64,512]{1,0:T(8,128)(2,1)S(1)} collective-permute-done((bf16[64,512]{1,0:T(8,128)(2,1)S(1)}, bf16[64,512]{1,0:T(8,128)(2,1)S(1)}, u32[]{:S(2)}, u32[]{:S(2)}) %collective-permute-start) | collective-permute-done | bytes 65568 | tf_op jit(solution)/shard_map/while/body/eval_jaxpr/ppermute | solution.py:9
  47.8 1.1 fusion.115
  50.6 5.7 %collective-permute-done = bf16[64,512]{1,0:T(8,128)(2,1)S(1)} collective-permute-done((bf16[64,512]{1,0:T(8,128)(2,1)S(1)}, bf16[64,512]{1,0:T(8,128)(2,1)S(1)}, u32[]{:S(2)}, u32[]{:S(2)}) %collective-permute-start) | collective-permute-done | bytes 65568 | tf_op jit(solution)/shard_map/while/body/eval_jaxpr/ppermute | solution.py:9
  56.6 1.1 fusion.115
  59.4 5.7 %collective-permute-done = bf16[64,512]{1,0:T(8,128)(2,1)S(1)} collective-permute-done((bf16[64,512]{1,0:T(8,128)(2,1)S(1)}, bf16[64,512]{1,0:T(8,128)(2,1)S(1)}, u32[]{:S(2)}, u32[]{:S(2)}) %collective-permute-start) | collective-permute-done | bytes 65568 | tf_op jit(solution)/shard_map/while/body/eval_jaxpr/ppermute | solution.py:9
  65.3 1.1 fusion.115
  68.2 5.7 %collective-permute-done = bf16[64,512]{1,0:T(8,128)(2,1)S(1)} collective-permute-done((bf16[64,512]{1,0:T(8,128)(2,1)S(1)}, bf16[64,512]{1,0:T(8,128)(2,1)S(1)}, u32[]{:S(2)}, u32[]{:S(2)}) %collective-permute-start) | collective-permute-done | bytes 65568 | tf_op jit(solution)/shard_map/while/body/eval_jaxpr/ppermute | solution.py:9
  74.1 1.1 fusion.115
  76.2 3.4 %all-to-all-start = ((bf16[64,4,128]{2,0,1:T(8,128)(2,1)}), bf16[64,4,128]{2,0,1:T(8,128)(2,1)S(1)}, u32[]{:S(2)}, u32[]{:S(2)}) async-start(bf16[64,4,128]{2,0,1:T(8,128)(2,1)} %copy.71), calls=%async_computation | async-start | bytes 131072 | tf_op jit(solution)/shard_map/all_to_all | solution.py:69
  80.5 3.3 %all-to-all-done = bf16[64,4,128]{2,0,1:T(8,128)(2,1)S(1)} async-done(((bf16[64,4,128]{2,0,1:T(8,128)(2,1)}), bf16[64,4,128]{2,0,1:T(8,128)(2,1)S(1)}, u32[]{:S(2)}, u32[]{:S(2)}) %all-to-all-start) | async-done | bytes 65568 | tf_op jit(solution)/shard_map/all_to_all | solution.py:69
  84.9 3.3 %all-to-all-start.1 = ((bf16[4,64,128]{2,1,0:T(8,128)(2,1)}), bf16[4,64,128]{2,1,0:T(8,128)(2,1)S(1)}, u32[]{:S(2)}, u32[]{:S(2)}) async-start(bf16[4,64,128]{2,1,0:T(8,128)(2,1)} %bitcast.30), calls=%async_computation.1 | async-start | bytes 131072 | tf_op jit(solution)/shard_map/all_to_all | solution.py:81
  89.9 2.4 %all-to-all-done.1 = bf16[4,64,128]{2,1,0:T(8,128)(2,1)S(1)} async-done(((bf16[4,64,128]{2,1,0:T(8,128)(2,1)}), bf16[4,64,128]{2,1,0:T(8,128)(2,1)S(1)}, u32[]{:S(2)}, u32[]{:S(2)}) %all-to-all-start.1) | async-done | bytes 65568 | tf_op jit(solution)/shard_map/all_to_all | solution.py:81
  93.9 58.6 %while.33 = (s32[]{:T(128)}, f32[64,4,128]{2,1,0:T(4,128)S(1)}, s32[]{:T(128)}, s32[8,4]{1,0:T(8,128)S(1)}, s32[8]{0:T(128)S(1)}, /*index=5*/bf16[32,128,128]{2,...) while((s32[]{:T(128)}, f32[64,4,128]{2,1,0:T(4,128)S(1)}, ...), condition=%wide.region_4.5_spmd, body=%wide.region_3.4_spmd.sunk | while | flops 8945742 | bytes 1245714 | solution.py:91
  96.5 5.2 %collective-permute-done.1 = f32[64,4,128]{2,1,0:T(4,128)S(1)} collective-permute-done((f32[64,4,128]{2,1,0:T(4,128)S(1)}, f32[64,4,128]{2,1,0:T(4,128)S(1)}, u32[]{:S(2)}, u32[]{:S(2)}) %collective-permute-start.1) | collective-permute-done | bytes 131104 | tf_op jit(solution)/shard_map/while/body/eval_jaxpr/ppermute | solution.py:9
  102.5 1.1 fusion.125
  104.8 5.2 %collective-permute-done.1 = f32[64,4,128]{2,1,0:T(4,128)S(1)} collective-permute-done((f32[64,4,128]{2,1,0:T(4,128)S(1)}, f32[64,4,128]{2,1,0:T(4,128)S(1)}, u32[]{:S(2)}, u32[]{:S(2)}) %collective-permute-start.1) | collective-permute-done | bytes 131104 | tf_op jit(solution)/shard_map/while/body/eval_jaxpr/ppermute | solution.py:9
  113.0 5.2 %collective-permute-done.1 = f32[64,4,128]{2,1,0:T(4,128)S(1)} collective-permute-done((f32[64,4,128]{2,1,0:T(4,128)S(1)}, f32[64,4,128]{2,1,0:T(4,128)S(1)}, u32[]{:S(2)}, u32[]{:S(2)}) %collective-permute-start.1) | collective-permute-done | bytes 131104 | tf_op jit(solution)/shard_map/while/body/eval_jaxpr/ppermute | solution.py:9
  121.2 5.1 %collective-permute-done.1 = f32[64,4,128]{2,1,0:T(4,128)S(1)} collective-permute-done((f32[64,4,128]{2,1,0:T(4,128)S(1)}, f32[64,4,128]{2,1,0:T(4,128)S(1)}, u32[]{:S(2)}, u32[]{:S(2)}) %collective-permute-start.1) | collective-permute-done | bytes 131104 | tf_op jit(solution)/shard_map/while/body/eval_jaxpr/ppermute | solution.py:9
  129.3 5.3 %collective-permute-done.1 = f32[64,4,128]{2,1,0:T(4,128)S(1)} collective-permute-done((f32[64,4,128]{2,1,0:T(4,128)S(1)}, f32[64,4,128]{2,1,0:T(4,128)S(1)}, u32[]{:S(2)}, u32[]{:S(2)}) %collective-permute-start.1) | collective-permute-done | bytes 131104 | tf_op jit(solution)/shard_map/while/body/eval_jaxpr/ppermute | solution.py:9
  137.7 6.3 %collective-permute-done.1 = f32[64,4,128]{2,1,0:T(4,128)S(1)} collective-permute-done((f32[64,4,128]{2,1,0:T(4,128)S(1)}, f32[64,4,128]{2,1,0:T(4,128)S(1)}, u32[]{:S(2)}, u32[]{:S(2)}) %collective-permute-start.1) | collective-permute-done | bytes 131104 | tf_op jit(solution)/shard_map/while/body/eval_jaxpr/ppermute | solution.py:9
  147.0 5.2 %collective-permute-done.1 = f32[64,4,128]{2,1,0:T(4,128)S(1)} collective-permute-done((f32[64,4,128]{2,1,0:T(4,128)S(1)}, f32[64,4,128]{2,1,0:T(4,128)S(1)}, u32[]{:S(2)}, u32[]{:S(2)}) %collective-permute-start.1) | collective-permute-done | bytes 131104 | tf_op jit(solution)/shard_map/while/body/eval_jaxpr/ppermute | solution.py:9
  153.2 65.3 %all-reduce.2.cloned.1.call-done = f32[256,256]{1,0:T(8,128)} async-done(((f32[256,256]{1,0:T(8,128)}), f32[256,256]{1,0:T(8,128)}) %all-reduce.2.cloned.1.call-update) | async-done | bytes 262160 | tf_op jit(solution)/shard_map/psum | solution.py:79
  218.5 1.7 copy.99
  (137 shorter events, 44.3 us)
Async XLA Ops:
  7.2 76.6 %copy-start = (bf16[256,256]{1,0:T(8,128)(2,1)S(1)}, bf16[256,256]{1,0:T(8,128)(2,1)}, u32[]{:S(2)}) copy-start(bf16[256,256]{1,0:T(8,128)(2,1)} %param.16) | copy-start | bytes 393220
  8.1 0.7 copy-start.2
  8.7 0.7 copy-start.3
  9.5 0.7 copy-start.4
  12.9 8.3 %collective-permute-start = (bf16[64,512]{1,0:T(8,128)(2,1)S(1)}, bf16[64,512]{1,0:T(8,128)(2,1)S(1)}, u32[]{:S(2)}, u32[]{:S(2)}) collective-permute-start(bf16[64,512]{1,0:T(8,128)(2,1)S(1)} %get-tuple-element.610), channel_id=1, source_target_pairs={{0,4},{4,8},{8,12},{12,16},{16,20},{20,24},{24,28},{28,0},{1,5},{5... | collective-permute-start | bytes 196616 | tf_op jit(solution)/shard_map/while/body/eval_jaxpr/ppermute | solution.py:9
  23.0 7.0 %collective-permute-start = (bf16[64,512]{1,0:T(8,128)(2,1)S(1)}, bf16[64,512]{1,0:T(8,128)(2,1)S(1)}, u32[]{:S(2)}, u32[]{:S(2)}) collective-permute-start(bf16[64,512]{1,0:T(8,128)(2,1)S(1)} %get-tuple-element.610), channel_id=1, source_target_pairs={{0,4},{4,8},{8,12},{12,16},{16,20},{20,24},{24,28},{28,0},{1,5},{5... | collective-permute-start | bytes 196616 | tf_op jit(solution)/shard_map/while/body/eval_jaxpr/ppermute | solution.py:9
  31.7 7.0 %collective-permute-start = (bf16[64,512]{1,0:T(8,128)(2,1)S(1)}, bf16[64,512]{1,0:T(8,128)(2,1)S(1)}, u32[]{:S(2)}, u32[]{:S(2)}) collective-permute-start(bf16[64,512]{1,0:T(8,128)(2,1)S(1)} %get-tuple-element.610), channel_id=1, source_target_pairs={{0,4},{4,8},{8,12},{12,16},{16,20},{20,24},{24,28},{28,0},{1,5},{5... | collective-permute-start | bytes 196616 | tf_op jit(solution)/shard_map/while/body/eval_jaxpr/ppermute | solution.py:9
  40.5 7.0 %collective-permute-start = (bf16[64,512]{1,0:T(8,128)(2,1)S(1)}, bf16[64,512]{1,0:T(8,128)(2,1)S(1)}, u32[]{:S(2)}, u32[]{:S(2)}) collective-permute-start(bf16[64,512]{1,0:T(8,128)(2,1)S(1)} %get-tuple-element.610), channel_id=1, source_target_pairs={{0,4},{4,8},{8,12},{12,16},{16,20},{20,24},{24,28},{28,0},{1,5},{5... | collective-permute-start | bytes 196616 | tf_op jit(solution)/shard_map/while/body/eval_jaxpr/ppermute | solution.py:9
  49.3 7.0 %collective-permute-start = (bf16[64,512]{1,0:T(8,128)(2,1)S(1)}, bf16[64,512]{1,0:T(8,128)(2,1)S(1)}, u32[]{:S(2)}, u32[]{:S(2)}) collective-permute-start(bf16[64,512]{1,0:T(8,128)(2,1)S(1)} %get-tuple-element.610), channel_id=1, source_target_pairs={{0,4},{4,8},{8,12},{12,16},{16,20},{20,24},{24,28},{28,0},{1,5},{5... | collective-permute-start | bytes 196616 | tf_op jit(solution)/shard_map/while/body/eval_jaxpr/ppermute | solution.py:9
  58.1 7.0 %collective-permute-start = (bf16[64,512]{1,0:T(8,128)(2,1)S(1)}, bf16[64,512]{1,0:T(8,128)(2,1)S(1)}, u32[]{:S(2)}, u32[]{:S(2)}) collective-permute-start(bf16[64,512]{1,0:T(8,128)(2,1)S(1)} %get-tuple-element.610), channel_id=1, source_target_pairs={{0,4},{4,8},{8,12},{12,16},{16,20},{20,24},{24,28},{28,0},{1,5},{5... | collective-permute-start | bytes 196616 | tf_op jit(solution)/shard_map/while/body/eval_jaxpr/ppermute | solution.py:9
  66.8 7.0 %collective-permute-start = (bf16[64,512]{1,0:T(8,128)(2,1)S(1)}, bf16[64,512]{1,0:T(8,128)(2,1)S(1)}, u32[]{:S(2)}, u32[]{:S(2)}) collective-permute-start(bf16[64,512]{1,0:T(8,128)(2,1)S(1)} %get-tuple-element.610), channel_id=1, source_target_pairs={{0,4},{4,8},{8,12},{12,16},{16,20},{20,24},{24,28},{28,0},{1,5},{5... | collective-permute-start | bytes 196616 | tf_op jit(solution)/shard_map/while/body/eval_jaxpr/ppermute | solution.py:9
  76.2 4.1 %copy-start.1 = (bf16[256,128]{1,0:T(8,128)(2,1)S(1)}, bf16[256,128]{1,0:T(8,128)(2,1)}, u32[]{:S(2)}) copy-start(bf16[256,128]{1,0:T(8,128)(2,1)} %param.17) | copy-start | bytes 196612
  76.2 7.5 %all-to-all-start = ((bf16[64,4,128]{2,0,1:T(8,128)(2,1)}), bf16[64,4,128]{2,0,1:T(8,128)(2,1)S(1)}, u32[]{:S(2)}, u32[]{:S(2)}) async-start(bf16[64,4,128]{2,0,1:T(8,128)(2,1)} %copy.71), calls=%async_computation | async-start | bytes 131072 | tf_op jit(solution)/shard_map/all_to_all | solution.py:69
  84.9 7.4 %all-to-all-start.1 = ((bf16[4,64,128]{2,1,0:T(8,128)(2,1)}), bf16[4,64,128]{2,1,0:T(8,128)(2,1)S(1)}, u32[]{:S(2)}, u32[]{:S(2)}) async-start(bf16[4,64,128]{2,1,0:T(8,128)(2,1)} %bitcast.30), calls=%async_computation.1 | async-start | bytes 131072 | tf_op jit(solution)/shard_map/all_to_all | solution.py:81
  88.2 130.3 %all-reduce.2.cloned.1.call-start = ((), (), s32[]{:S(2)}) async-start(), calls=%async_computation.2 | async-start | bytes 524288 | tf_op jit(solution)/shard_map/psum | solution.py:79
  93.9 7.9 %collective-permute-start.1 = (f32[64,4,128]{2,1,0:T(4,128)S(1)}, f32[64,4,128]{2,1,0:T(4,128)S(1)}, u32[]{:S(2)}, u32[]{:S(2)}) collective-permute-start(f32[64,4,128]{2,1,0:T(4,128)S(1)} %get-tuple-element.652), channel_id=1, source_target_pairs={{0,4},{4,8},{8,12},{12,16},{16,20},{20,24},{24,28},{28,0},{1,5},{5... | collective-permute-start | bytes 393224 | tf_op jit(solution)/shard_map/while/body/eval_jaxpr/ppermute | solution.py:9
  102.1 7.9 %collective-permute-start.1 = (f32[64,4,128]{2,1,0:T(4,128)S(1)}, f32[64,4,128]{2,1,0:T(4,128)S(1)}, u32[]{:S(2)}, u32[]{:S(2)}) collective-permute-start(f32[64,4,128]{2,1,0:T(4,128)S(1)} %get-tuple-element.652), channel_id=1, source_target_pairs={{0,4},{4,8},{8,12},{12,16},{16,20},{20,24},{24,28},{28,0},{1,5},{5... | collective-permute-start | bytes 393224 | tf_op jit(solution)/shard_map/while/body/eval_jaxpr/ppermute | solution.py:9
  110.4 7.9 %collective-permute-start.1 = (f32[64,4,128]{2,1,0:T(4,128)S(1)}, f32[64,4,128]{2,1,0:T(4,128)S(1)}, u32[]{:S(2)}, u32[]{:S(2)}) collective-permute-start(f32[64,4,128]{2,1,0:T(4,128)S(1)} %get-tuple-element.652), channel_id=1, source_target_pairs={{0,4},{4,8},{8,12},{12,16},{16,20},{20,24},{24,28},{28,0},{1,5},{5... | collective-permute-start | bytes 393224 | tf_op jit(solution)/shard_map/while/body/eval_jaxpr/ppermute | solution.py:9
  118.6 7.7 %collective-permute-start.1 = (f32[64,4,128]{2,1,0:T(4,128)S(1)}, f32[64,4,128]{2,1,0:T(4,128)S(1)}, u32[]{:S(2)}, u32[]{:S(2)}) collective-permute-start(f32[64,4,128]{2,1,0:T(4,128)S(1)} %get-tuple-element.652), channel_id=1, source_target_pairs={{0,4},{4,8},{8,12},{12,16},{16,20},{20,24},{24,28},{28,0},{1,5},{5... | collective-permute-start | bytes 393224 | tf_op jit(solution)/shard_map/while/body/eval_jaxpr/ppermute | solution.py:9
  126.7 8.0 %collective-permute-start.1 = (f32[64,4,128]{2,1,0:T(4,128)S(1)}, f32[64,4,128]{2,1,0:T(4,128)S(1)}, u32[]{:S(2)}, u32[]{:S(2)}) collective-permute-start(f32[64,4,128]{2,1,0:T(4,128)S(1)} %get-tuple-element.652), channel_id=1, source_target_pairs={{0,4},{4,8},{8,12},{12,16},{16,20},{20,24},{24,28},{28,0},{1,5},{5... | collective-permute-start | bytes 393224 | tf_op jit(solution)/shard_map/while/body/eval_jaxpr/ppermute | solution.py:9
  135.0 8.9 %collective-permute-start.1 = (f32[64,4,128]{2,1,0:T(4,128)S(1)}, f32[64,4,128]{2,1,0:T(4,128)S(1)}, u32[]{:S(2)}, u32[]{:S(2)}) collective-permute-start(f32[64,4,128]{2,1,0:T(4,128)S(1)} %get-tuple-element.652), channel_id=1, source_target_pairs={{0,4},{4,8},{8,12},{12,16},{16,20},{20,24},{24,28},{28,0},{1,5},{5... | collective-permute-start | bytes 393224 | tf_op jit(solution)/shard_map/while/body/eval_jaxpr/ppermute | solution.py:9
  144.3 7.8 %collective-permute-start.1 = (f32[64,4,128]{2,1,0:T(4,128)S(1)}, f32[64,4,128]{2,1,0:T(4,128)S(1)}, u32[]{:S(2)}, u32[]{:S(2)}) collective-permute-start(f32[64,4,128]{2,1,0:T(4,128)S(1)} %get-tuple-element.652), channel_id=1, source_target_pairs={{0,4},{4,8},{8,12},{12,16},{16,20},{20,24},{24,28},{28,0},{1,5},{5... | collective-permute-start | bytes 393224 | tf_op jit(solution)/shard_map/while/body/eval_jaxpr/ppermute | solution.py:9
Sparse Core Ops, SparseCore 0:
  95.1 123.3 all-reduce.1
where the time goes:
time: 228 us; the launch traced here: 227 us
  waiting for transfers between devices  147 us (64%)
  matrix products  27.7 us (12%)
  local copies, waits for them, and re-layouts  16.8 us (7%)
  between operations  14.2 us (6%)
  starting transfers between devices  10.5 us (5%)
  other arithmetic  10.4 us (5%)
    ppermute x14, waiting for transfers between devices, passed_along(): return lax.ppermute(x, axis, [(i, (i + by) % count) for i in range(count)])  75.5 us
    psum x1, waiting for transfers between devices, per_device(): grad_weight = lax.psum(weight_part, ('node', 'feat'))  65.3 us
    convert_element_type x16, other arithmetic, select_pair(): live = (jnp.arange(slots) < number).astype(jnp.float32)  10.4 us
    dynamic_slice x15, local copies, waits for them, and re-layouts, select_pair(): number = lax.dynamic_index_in_dim(tile_counts, source, 0, keepdims=False)  8.87 us
    dot_general x8, matrix products, add_forward(): jnp.einsum('fsm,sjm->fsj', chosen, values, preferred_element_type=jnp.flo...  8.64 us
    dot_general x8, matrix products, add_backward(): jnp.einsum('fsj,sjm->fsm', chosen, values, preferred_element_type=jnp.flo...  8.47 us
    unnamed x15, local copies, waits for them, and re-layouts  5.78 us
  transfers between devices with their start and end apart: 17, of which 17 were waited for; matrix products, arithmetic and copies ran while one was open for 15% of the time, Pallas kernels for 0%

commit v1 on v0

--- a/solution.py
+++ b/solution.py
@@ -76,7 +76,7 @@
     weight_part = lax.dot_general(
         full_rows, dpre, (((1,), (1,)), ((), ())), preferred_element_type=jnp.float32
     )
-    grad_weight = lax.psum(weight_part, ("node", "feat"))
+    grad_weight = lax.psum(lax.psum(weight_part, "feat"), "node")
     dagg = jnp.dot(weight, dpre, preferred_element_type=jnp.float32).astype(jnp.bfloat16)
     grad_slices = lax.all_to_all(dagg, "feat", split_axis=0, concat_axis=1, tiled=True)
     grad_blocks = grad_slices.reshape(slice_width, block_count, tile_side)

time: 228 us -> 208 us (0.912)
  waiting for transfers between devices: 147 us -> 125 us
    psum x1 -> x2, waiting for transfers between devices: 65.3 us -> 44.1 us  [per_device(): grad_weight = lax.psum(lax.psum(weight_part, 'feat'), 'node')]
  transfers between devices with their start and end apart: 17 -> 18, of which waited for: 17 -> 18; matrix products, arithmetic and copies ran while one was open for 15% -> 16% of each run, Pallas kernels for 0% -> 0%
where the time goes in v1:
time: 208 us; the launch traced here: 207 us
  waiting for transfers between devices  125 us (60%)
  matrix products  27.7 us (13%)
  local copies, waits for them, and re-layouts  16.8 us (8%)
  between operations  14.2 us (7%)
  starting transfers between devices  12 us (6%)
  other arithmetic  10.4 us (5%)
    ppermute x14, waiting for transfers between devices, passed_along(): return lax.ppermute(x, axis, [(i, (i + by) % count) for i in range(count)])  75.2 us
    psum x2, waiting for transfers between devices, per_device(): grad_weight = lax.psum(lax.psum(weight_part, 'feat'), 'node')  44.1 us
    convert_element_type x16, other arithmetic, select_pair(): live = (jnp.arange(slots) < number).astype(jnp.float32)  10.4 us
    dynamic_slice x15, local copies, waits for them, and re-layouts, select_pair(): number = lax.dynamic_index_in_dim(tile_counts, source, 0, keepdims=False)  8.87 us
    dot_general x8, matrix products, add_forward(): jnp.einsum('fsm,sjm->fsj', chosen, values, preferred_element_type=jnp.flo...  8.64 us
    dot_general x8, matrix products, add_backward(): jnp.einsum('fsj,sjm->fsm', chosen, values, preferred_element_type=jnp.flo...  8.48 us
    unnamed x15, local copies, waits for them, and re-layouts  5.78 us
    ppermute x14, starting transfers between devices, passed_along(): return lax.ppermute(x, axis, [(i, (i + by) % count) for i in range(count)])  5.21 us
  transfers between devices with their start and end apart: 18, of which 18 were waited for; matrix products, arithmetic and copies ran while one was open for 16% of the time, Pallas kernels for 0%

profile of v1, /device:TPU:0, one launch (start us, length us, event | category | flops | bytes accessed | tf_op | source)
XLA Modules:
  0.0 207.0 jit_solution(7341547594399808723)
XLA Ops:
  11.7 1.1 fusion.47
  12.9 62.7 %while.32 = (s32[]{:T(128)}, f32[64,4,128]{2,1,0:T(4,128)S(1)}, bf16[64,512]{1,0:T(8,128)(2,1)S(1)}, s32[]{:T(128)}, s32[8,4]{1,0:T(8,128)S(1)}, /*index=5*/s32[...) while((s32[]{:T(128)}, f32[64,4,128]{2,1,0:T(4,128)S(1)}, ...), condition=%wide.region_1.2_spmd, body=%wide.region_0.1_spmd.sunk | while | flops 8945741 | bytes 1245694 | solution.py:67
  12.9 3.0 %collective-permute-start = (bf16[64,512]{1,0:T(8,128)(2,1)S(1)}, bf16[64,512]{1,0:T(8,128)(2,1)S(1)}, u32[]{:S(2)}, u32[]{:S(2)}) collective-permute-start(bf16[64,512]{1,0:T(8,128)(2,1)S(1)} %get-tuple-element.610), channel_id=1, source_target_pairs={{0,4},{4,8},{8,12},{12,16},{16,20},{20,24},{24,28},{28,0},{1,5},{5... | collective-permute-start | bytes 196616 | tf_op jit(solution)/shard_map/while/body/eval_jaxpr/ppermute | solution.py:9
  17.2 4.0 %collective-permute-done = bf16[64,512]{1,0:T(8,128)(2,1)S(1)} collective-permute-done((bf16[64,512]{1,0:T(8,128)(2,1)S(1)}, bf16[64,512]{1,0:T(8,128)(2,1)S(1)}, u32[]{:S(2)}, u32[]{:S(2)}) %collective-permute-start) | collective-permute-done | bytes 65568 | tf_op jit(solution)/shard_map/while/body/eval_jaxpr/ppermute | solution.py:9
  21.5 1.1 fusion.115
  24.3 5.7 %collective-permute-done = bf16[64,512]{1,0:T(8,128)(2,1)S(1)} collective-permute-done((bf16[64,512]{1,0:T(8,128)(2,1)S(1)}, bf16[64,512]{1,0:T(8,128)(2,1)S(1)}, u32[]{:S(2)}, u32[]{:S(2)}) %collective-permute-start) | collective-permute-done | bytes 65568 | tf_op jit(solution)/shard_map/while/body/eval_jaxpr/ppermute | solution.py:9
  30.3 1.1 fusion.115
  33.1 5.7 %collective-permute-done = bf16[64,512]{1,0:T(8,128)(2,1)S(1)} collective-permute-done((bf16[64,512]{1,0:T(8,128)(2,1)S(1)}, bf16[64,512]{1,0:T(8,128)(2,1)S(1)}, u32[]{:S(2)}, u32[]{:S(2)}) %collective-permute-start) | collective-permute-done | bytes 65568 | tf_op jit(solution)/shard_map/while/body/eval_jaxpr/ppermute | solution.py:9
  39.0 1.1 fusion.115
  41.9 5.7 %collective-permute-done = bf16[64,512]{1,0:T(8,128)(2,1)S(1)} collective-permute-done((bf16[64,512]{1,0:T(8,128)(2,1)S(1)}, bf16[64,512]{1,0:T(8,128)(2,1)S(1)}, u32[]{:S(2)}, u32[]{:S(2)}) %collective-permute-start) | collective-permute-done | bytes 65568 | tf_op jit(solution)/shard_map/while/body/eval_jaxpr/ppermute | solution.py:9
  47.8 1.1 fusion.115
  50.6 5.7 %collective-permute-done = bf16[64,512]{1,0:T(8,128)(2,1)S(1)} collective-permute-done((bf16[64,512]{1,0:T(8,128)(2,1)S(1)}, bf16[64,512]{1,0:T(8,128)(2,1)S(1)}, u32[]{:S(2)}, u32[]{:S(2)}) %collective-permute-start) | collective-permute-done | bytes 65568 | tf_op jit(solution)/shard_map/while/body/eval_jaxpr/ppermute | solution.py:9
  56.6 1.1 fusion.115
  59.4 5.7 %collective-permute-done = bf16[64,512]{1,0:T(8,128)(2,1)S(1)} collective-permute-done((bf16[64,512]{1,0:T(8,128)(2,1)S(1)}, bf16[64,512]{1,0:T(8,128)(2,1)S(1)}, u32[]{:S(2)}, u32[]{:S(2)}) %collective-permute-start) | collective-permute-done | bytes 65568 | tf_op jit(solution)/shard_map/while/body/eval_jaxpr/ppermute | solution.py:9
  68.2 5.7 %collective-permute-done = bf16[64,512]{1,0:T(8,128)(2,1)S(1)} collective-permute-done((bf16[64,512]{1,0:T(8,128)(2,1)S(1)}, bf16[64,512]{1,0:T(8,128)(2,1)S(1)}, u32[]{:S(2)}, u32[]{:S(2)}) %collective-permute-start) | collective-permute-done | bytes 65568 | tf_op jit(solution)/shard_map/while/body/eval_jaxpr/ppermute | solution.py:9
  74.1 1.1 fusion.115
  76.2 3.4 %all-to-all-start = ((bf16[64,4,128]{2,0,1:T(8,128)(2,1)}), bf16[64,4,128]{2,0,1:T(8,128)(2,1)S(1)}, u32[]{:S(2)}, u32[]{:S(2)}) async-start(bf16[64,4,128]{2,0,1:T(8,128)(2,1)} %copy.71), calls=%async_computation | async-start | bytes 131072 | tf_op jit(solution)/shard_map/all_to_all | solution.py:69
  80.5 3.3 %all-to-all-done = bf16[64,4,128]{2,0,1:T(8,128)(2,1)S(1)} async-done(((bf16[64,4,128]{2,0,1:T(8,128)(2,1)}), bf16[64,4,128]{2,0,1:T(8,128)(2,1)S(1)}, u32[]{:S(2)}, u32[]{:S(2)}) %all-to-all-start) | async-done | bytes 65568 | tf_op jit(solution)/shard_map/all_to_all | solution.py:69
  84.9 3.3 %all-to-all-start.1 = ((bf16[4,64,128]{2,1,0:T(8,128)(2,1)}), bf16[4,64,128]{2,1,0:T(8,128)(2,1)S(1)}, u32[]{:S(2)}, u32[]{:S(2)}) async-start(bf16[4,64,128]{2,1,0:T(8,128)(2,1)} %bitcast.30), calls=%async_computation.1 | async-start | bytes 131072 | tf_op jit(solution)/shard_map/all_to_all | solution.py:81
  90.0 2.4 %all-to-all-done.1 = bf16[4,64,128]{2,1,0:T(8,128)(2,1)S(1)} async-done(((bf16[4,64,128]{2,1,0:T(8,128)(2,1)}), bf16[4,64,128]{2,1,0:T(8,128)(2,1)S(1)}, u32[]{:S(2)}, u32[]{:S(2)}) %all-to-all-start.1) | async-done | bytes 65568 | tf_op jit(solution)/shard_map/all_to_all | solution.py:81
  93.9 27.9 %all-reduce.3.cloned.1.call-done = f32[256,256]{1,0:T(8,128)} async-done(((f32[256,256]{1,0:T(8,128)}), f32[256,256]{1,0:T(8,128)}) %all-reduce.3.cloned.1.call-update) | async-done | bytes 262160 | tf_op jit(solution)/shard_map/psum | solution.py:79
  121.7 59.8 %while.33 = (s32[]{:T(128)}, f32[64,4,128]{2,1,0:T(4,128)S(1)}, s32[]{:T(128)}, s32[8,4]{1,0:T(8,128)S(1)}, s32[8]{0:T(128)S(1)}, /*index=5*/bf16[32,128,128]{2,...) while((s32[]{:T(128)}, f32[64,4,128]{2,1,0:T(4,128)S(1)}, ...), condition=%wide.region_5.6_spmd, body=%wide.region_4.5_spmd.sunk | while | flops 8945742 | bytes 1245714 | solution.py:91
  121.7 1.5 collective-permute-start.1
  125.8 3.6 %collective-permute-done.1 = f32[64,4,128]{2,1,0:T(4,128)S(1)} collective-permute-done((f32[64,4,128]{2,1,0:T(4,128)S(1)}, f32[64,4,128]{2,1,0:T(4,128)S(1)}, u32[]{:S(2)}, u32[]{:S(2)}) %collective-permute-start.1) | collective-permute-done | bytes 131104 | tf_op jit(solution)/shard_map/while/body/eval_jaxpr/ppermute | solution.py:9
  132.5 5.5 %collective-permute-done.1 = f32[64,4,128]{2,1,0:T(4,128)S(1)} collective-permute-done((f32[64,4,128]{2,1,0:T(4,128)S(1)}, f32[64,4,128]{2,1,0:T(4,128)S(1)}, u32[]{:S(2)}, u32[]{:S(2)}) %collective-permute-start.1) | collective-permute-done | bytes 131104 | tf_op jit(solution)/shard_map/while/body/eval_jaxpr/ppermute | solution.py:9
  141.0 5.0 %collective-permute-done.1 = f32[64,4,128]{2,1,0:T(4,128)S(1)} collective-permute-done((f32[64,4,128]{2,1,0:T(4,128)S(1)}, f32[64,4,128]{2,1,0:T(4,128)S(1)}, u32[]{:S(2)}, u32[]{:S(2)}) %collective-permute-start.1) | collective-permute-done | bytes 131104 | tf_op jit(solution)/shard_map/while/body/eval_jaxpr/ppermute | solution.py:9
  149.1 5.8 %collective-permute-done.1 = f32[64,4,128]{2,1,0:T(4,128)S(1)} collective-permute-done((f32[64,4,128]{2,1,0:T(4,128)S(1)}, f32[64,4,128]{2,1,0:T(4,128)S(1)}, u32[]{:S(2)}, u32[]{:S(2)}) %collective-permute-start.1) | collective-permute-done | bytes 131104 | tf_op jit(solution)/shard_map/while/body/eval_jaxpr/ppermute | solution.py:9
  157.9 6.4 %collective-permute-done.1 = f32[64,4,128]{2,1,0:T(4,128)S(1)} collective-permute-done((f32[64,4,128]{2,1,0:T(4,128)S(1)}, f32[64,4,128]{2,1,0:T(4,128)S(1)}, u32[]{:S(2)}, u32[]{:S(2)}) %collective-permute-start.1) | collective-permute-done | bytes 131104 | tf_op jit(solution)/shard_map/while/body/eval_jaxpr/ppermute | solution.py:9
  167.3 5.7 %collective-permute-done.1 = f32[64,4,128]{2,1,0:T(4,128)S(1)} collective-permute-done((f32[64,4,128]{2,1,0:T(4,128)S(1)}, f32[64,4,128]{2,1,0:T(4,128)S(1)}, u32[]{:S(2)}, u32[]{:S(2)}) %collective-permute-start.1) | collective-permute-done | bytes 131104 | tf_op jit(solution)/shard_map/while/body/eval_jaxpr/ppermute | solution.py:9
  176.1 5.1 %collective-permute-done.1 = f32[64,4,128]{2,1,0:T(4,128)S(1)} collective-permute-done((f32[64,4,128]{2,1,0:T(4,128)S(1)}, f32[64,4,128]{2,1,0:T(4,128)S(1)}, u32[]{:S(2)}, u32[]{:S(2)}) %collective-permute-start.1) | collective-permute-done | bytes 131104 | tf_op jit(solution)/shard_map/while/body/eval_jaxpr/ppermute | solution.py:9
  182.2 16.3 %all-reduce.5.cloned.1.call-done = f32[256,256]{1,0:T(8,128)} async-done(((f32[256,256]{1,0:T(8,128)}), f32[256,256]{1,0:T(8,128)}) %all-reduce.5.cloned.1.call-update) | async-done | bytes 262160 | tf_op jit(solution)/shard_map/psum | solution.py:79
  198.5 1.7 copy.100
  (140 shorter events, 46.4 us)
Async XLA Ops:
  7.2 76.6 %copy-start = (bf16[256,256]{1,0:T(8,128)(2,1)S(1)}, bf16[256,256]{1,0:T(8,128)(2,1)}, u32[]{:S(2)}) copy-start(bf16[256,256]{1,0:T(8,128)(2,1)} %param.16) | copy-start | bytes 393220
  8.1 0.7 copy-start.2
  8.7 0.7 copy-start.3
  9.5 0.7 copy-start.4
  12.9 8.3 %collective-permute-start = (bf16[64,512]{1,0:T(8,128)(2,1)S(1)}, bf16[64,512]{1,0:T(8,128)(2,1)S(1)}, u32[]{:S(2)}, u32[]{:S(2)}) collective-permute-start(bf16[64,512]{1,0:T(8,128)(2,1)S(1)} %get-tuple-element.610), channel_id=1, source_target_pairs={{0,4},{4,8},{8,12},{12,16},{16,20},{20,24},{24,28},{28,0},{1,5},{5... | collective-permute-start | bytes 196616 | tf_op jit(solution)/shard_map/while/body/eval_jaxpr/ppermute | solution.py:9
  23.0 7.0 %collective-permute-start = (bf16[64,512]{1,0:T(8,128)(2,1)S(1)}, bf16[64,512]{1,0:T(8,128)(2,1)S(1)}, u32[]{:S(2)}, u32[]{:S(2)}) collective-permute-start(bf16[64,512]{1,0:T(8,128)(2,1)S(1)} %get-tuple-element.610), channel_id=1, source_target_pairs={{0,4},{4,8},{8,12},{12,16},{16,20},{20,24},{24,28},{28,0},{1,5},{5... | collective-permute-start | bytes 196616 | tf_op jit(solution)/shard_map/while/body/eval_jaxpr/ppermute | solution.py:9
  31.7 7.0 %collective-permute-start = (bf16[64,512]{1,0:T(8,128)(2,1)S(1)}, bf16[64,512]{1,0:T(8,128)(2,1)S(1)}, u32[]{:S(2)}, u32[]{:S(2)}) collective-permute-start(bf16[64,512]{1,0:T(8,128)(2,1)S(1)} %get-tuple-element.610), channel_id=1, source_target_pairs={{0,4},{4,8},{8,12},{12,16},{16,20},{20,24},{24,28},{28,0},{1,5},{5... | collective-permute-start | bytes 196616 | tf_op jit(solution)/shard_map/while/body/eval_jaxpr/ppermute | solution.py:9
  40.5 7.0 %collective-permute-start = (bf16[64,512]{1,0:T(8,128)(2,1)S(1)}, bf16[64,512]{1,0:T(8,128)(2,1)S(1)}, u32[]{:S(2)}, u32[]{:S(2)}) collective-permute-start(bf16[64,512]{1,0:T(8,128)(2,1)S(1)} %get-tuple-element.610), channel_id=1, source_target_pairs={{0,4},{4,8},{8,12},{12,16},{16,20},{20,24},{24,28},{28,0},{1,5},{5... | collective-permute-start | bytes 196616 | tf_op jit(solution)/shard_map/while/body/eval_jaxpr/ppermute | solution.py:9
  49.3 7.0 %collective-permute-start = (bf16[64,512]{1,0:T(8,128)(2,1)S(1)}, bf16[64,512]{1,0:T(8,128)(2,1)S(1)}, u32[]{:S(2)}, u32[]{:S(2)}) collective-permute-start(bf16[64,512]{1,0:T(8,128)(2,1)S(1)} %get-tuple-element.610), channel_id=1, source_target_pairs={{0,4},{4,8},{8,12},{12,16},{16,20},{20,24},{24,28},{28,0},{1,5},{5... | collective-permute-start | bytes 196616 | tf_op jit(solution)/shard_map/while/body/eval_jaxpr/ppermute | solution.py:9
  58.1 7.0 %collective-permute-start = (bf16[64,512]{1,0:T(8,128)(2,1)S(1)}, bf16[64,512]{1,0:T(8,128)(2,1)S(1)}, u32[]{:S(2)}, u32[]{:S(2)}) collective-permute-start(bf16[64,512]{1,0:T(8,128)(2,1)S(1)} %get-tuple-element.610), channel_id=1, source_target_pairs={{0,4},{4,8},{8,12},{12,16},{16,20},{20,24},{24,28},{28,0},{1,5},{5... | collective-permute-start | bytes 196616 | tf_op jit(solution)/shard_map/while/body/eval_jaxpr/ppermute | solution.py:9
  66.8 7.0 %collective-permute-start = (bf16[64,512]{1,0:T(8,128)(2,1)S(1)}, bf16[64,512]{1,0:T(8,128)(2,1)S(1)}, u32[]{:S(2)}, u32[]{:S(2)}) collective-permute-start(bf16[64,512]{1,0:T(8,128)(2,1)S(1)} %get-tuple-element.610), channel_id=1, source_target_pairs={{0,4},{4,8},{8,12},{12,16},{16,20},{20,24},{24,28},{28,0},{1,5},{5... | collective-permute-start | bytes 196616 | tf_op jit(solution)/shard_map/while/body/eval_jaxpr/ppermute | solution.py:9
  76.2 4.1 %copy-start.1 = (bf16[256,128]{1,0:T(8,128)(2,1)S(1)}, bf16[256,128]{1,0:T(8,128)(2,1)}, u32[]{:S(2)}) copy-start(bf16[256,128]{1,0:T(8,128)(2,1)} %param.17) | copy-start | bytes 196612
  76.2 7.5 %all-to-all-start = ((bf16[64,4,128]{2,0,1:T(8,128)(2,1)}), bf16[64,4,128]{2,0,1:T(8,128)(2,1)S(1)}, u32[]{:S(2)}, u32[]{:S(2)}) async-start(bf16[64,4,128]{2,0,1:T(8,128)(2,1)} %copy.71), calls=%async_computation | async-start | bytes 131072 | tf_op jit(solution)/shard_map/all_to_all | solution.py:69
  84.9 7.4 %all-to-all-start.1 = ((bf16[4,64,128]{2,1,0:T(8,128)(2,1)}), bf16[4,64,128]{2,1,0:T(8,128)(2,1)S(1)}, u32[]{:S(2)}, u32[]{:S(2)}) async-start(bf16[4,64,128]{2,1,0:T(8,128)(2,1)} %bitcast.30), calls=%async_computation.1 | async-start | bytes 131072 | tf_op jit(solution)/shard_map/all_to_all | solution.py:81
  88.2 33.5 %all-reduce.3.cloned.1.call-start = ((), (), s32[]{:S(2)}) async-start(), calls=%async_computation.2 | async-start | bytes 524288 | tf_op jit(solution)/shard_map/psum | solution.py:79
  89.9 108.6 %all-reduce.5.cloned.1.call-start = ((), (), s32[]{:S(2)}) async-start(), calls=%async_computation.3 | async-start | bytes 524288 | tf_op jit(solution)/shard_map/psum | solution.py:79
  121.7 7.7 %collective-permute-start.1 = (f32[64,4,128]{2,1,0:T(4,128)S(1)}, f32[64,4,128]{2,1,0:T(4,128)S(1)}, u32[]{:S(2)}, u32[]{:S(2)}) collective-permute-start(f32[64,4,128]{2,1,0:T(4,128)S(1)} %get-tuple-element.652), channel_id=1, source_target_pairs={{0,4},{4,8},{8,12},{12,16},{16,20},{20,24},{24,28},{28,0},{1,5},{5... | collective-permute-start | bytes 393224 | tf_op jit(solution)/shard_map/while/body/eval_jaxpr/ppermute | solution.py:9
  129.8 8.2 %collective-permute-start.1 = (f32[64,4,128]{2,1,0:T(4,128)S(1)}, f32[64,4,128]{2,1,0:T(4,128)S(1)}, u32[]{:S(2)}, u32[]{:S(2)}) collective-permute-start(f32[64,4,128]{2,1,0:T(4,128)S(1)} %get-tuple-element.652), channel_id=1, source_target_pairs={{0,4},{4,8},{8,12},{12,16},{16,20},{20,24},{24,28},{28,0},{1,5},{5... | collective-permute-start | bytes 393224 | tf_op jit(solution)/shard_map/while/body/eval_jaxpr/ppermute | solution.py:9
  138.4 7.7 %collective-permute-start.1 = (f32[64,4,128]{2,1,0:T(4,128)S(1)}, f32[64,4,128]{2,1,0:T(4,128)S(1)}, u32[]{:S(2)}, u32[]{:S(2)}) collective-permute-start(f32[64,4,128]{2,1,0:T(4,128)S(1)} %get-tuple-element.652), channel_id=1, source_target_pairs={{0,4},{4,8},{8,12},{12,16},{16,20},{20,24},{24,28},{28,0},{1,5},{5... | collective-permute-start | bytes 393224 | tf_op jit(solution)/shard_map/while/body/eval_jaxpr/ppermute | solution.py:9
  146.5 8.4 %collective-permute-start.1 = (f32[64,4,128]{2,1,0:T(4,128)S(1)}, f32[64,4,128]{2,1,0:T(4,128)S(1)}, u32[]{:S(2)}, u32[]{:S(2)}) collective-permute-start(f32[64,4,128]{2,1,0:T(4,128)S(1)} %get-tuple-element.652), channel_id=1, source_target_pairs={{0,4},{4,8},{8,12},{12,16},{16,20},{20,24},{24,28},{28,0},{1,5},{5... | collective-permute-start | bytes 393224 | tf_op jit(solution)/shard_map/while/body/eval_jaxpr/ppermute | solution.py:9
  155.3 9.0 %collective-permute-start.1 = (f32[64,4,128]{2,1,0:T(4,128)S(1)}, f32[64,4,128]{2,1,0:T(4,128)S(1)}, u32[]{:S(2)}, u32[]{:S(2)}) collective-permute-start(f32[64,4,128]{2,1,0:T(4,128)S(1)} %get-tuple-element.652), channel_id=1, source_target_pairs={{0,4},{4,8},{8,12},{12,16},{16,20},{20,24},{24,28},{28,0},{1,5},{5... | collective-permute-start | bytes 393224 | tf_op jit(solution)/shard_map/while/body/eval_jaxpr/ppermute | solution.py:9
  164.7 8.4 %collective-permute-start.1 = (f32[64,4,128]{2,1,0:T(4,128)S(1)}, f32[64,4,128]{2,1,0:T(4,128)S(1)}, u32[]{:S(2)}, u32[]{:S(2)}) collective-permute-start(f32[64,4,128]{2,1,0:T(4,128)S(1)} %get-tuple-element.652), channel_id=1, source_target_pairs={{0,4},{4,8},{8,12},{12,16},{16,20},{20,24},{24,28},{28,0},{1,5},{5... | collective-permute-start | bytes 393224 | tf_op jit(solution)/shard_map/while/body/eval_jaxpr/ppermute | solution.py:9
  173.4 7.8 %collective-permute-start.1 = (f32[64,4,128]{2,1,0:T(4,128)S(1)}, f32[64,4,128]{2,1,0:T(4,128)S(1)}, u32[]{:S(2)}, u32[]{:S(2)}) collective-permute-start(f32[64,4,128]{2,1,0:T(4,128)S(1)} %get-tuple-element.652), channel_id=1, source_target_pairs={{0,4},{4,8},{8,12},{12,16},{16,20},{20,24},{24,28},{28,0},{1,5},{5... | collective-permute-start | bytes 393224 | tf_op jit(solution)/shard_map/while/body/eval_jaxpr/ppermute | solution.py:9
Sparse Core Ops, SparseCore 0:
  92.0 29.6 all-reduce.2
  125.4 73.0 all-reduce.4
